TPU v7x, 32 devices: a whole 2x2x4 slice. The times are simulated.
32 devices in a mesh: shard: 2 (over x), ctx: 4 (over z), tensor: 4 (over y, core).
Axes of the slice: x: 2, y: 2, z: 4, core: 2. Of those that a mesh axis runs over, the one named last changes fastest.
Arguments:
- inputs: bfloat16 [1024, 8, 1024], P('ctx', 'shard'), may hold values from -6 to 6
- time_features: bfloat16 [8, 256], P('shard'), may hold values from -1 to 1
- valid_mask: int32 [1024, 8], P('ctx', 'shard'), may hold values from 0 to 1, as said below
- teacher: bfloat16 [1024, 8, 1024], P('ctx', 'shard'), may hold values from -6 to 6
- w_time: bfloat16 [256, 1024], replicated, may hold values from -0.375 to 0.375
- b_time: float32 [1024], replicated, may hold values from -2 to 2
- w_query: bfloat16 [1024, 1024], P('shard', 'tensor'), may hold values from -0.1875 to 0.1875
- b_query: float32 [1024], P('tensor'), may hold values from -2 to 2
- w_key: bfloat16 [1024, 1024], P('shard', 'tensor'), may hold values from -0.1875 to 0.1875
- w_value: bfloat16 [1024, 1024], P('shard', 'tensor'), may hold values from -0.1875 to 0.1875
- b_value: float32 [1024], P('tensor'), may hold values from -0.3 to 0.3
- w_output: bfloat16 [1024, 1024], P('shard', 'tensor'), may hold values from -1.5 to 1.5
- b_output: float32 [1024], replicated, may hold values from -2 to 2
- gain_one: float32 [1024], replicated, may hold values from 0.5 to 1.5
- shift_one: float32 [1024], replicated, may hold values from -2 to 2
- w_hidden: bfloat16 [1024, 4096], P('shard', 'tensor'), may hold values from -0.1875 to 0.1875
- b_hidden: float32 [4096], P('tensor'), may hold values from -2 to 2
- w_down: bfloat16 [1024, 4096], P('shard', 'tensor'), may hold values from -0.09375 to 0.09375
- b_down: float32 [1024], replicated, may hold values from -2 to 2
- gain_two: float32 [1024], replicated, may hold values from 0.5 to 1.5
- shift_two: float32 [1024], replicated, may hold values from -2 to 2
Outputs:
- layer_out: bfloat16 [1024, 8, 1024], P('ctx', 'shard')
- loss: float32 [], replicated
- grad_inputs: float32 [1024, 8, 1024], P('ctx', 'shard')
- grad_w_time: float32 [256, 1024], replicated
- grad_b_time: float32 [1024], replicated
- grad_w_query: float32 [1024, 1024], P(('shard', 'ctx'), 'tensor')
- grad_b_query: float32 [1024], P('tensor')
- grad_w_key: float32 [1024, 1024], P(('shard', 'ctx'), 'tensor')
- grad_w_value: float32 [1024, 1024], P(('shard', 'ctx'), 'tensor')
- grad_b_value: float32 [1024], P('tensor')
- grad_w_output: float32 [1024, 1024], P(('shard', 'ctx'), 'tensor')
- grad_b_output: float32 [1024], replicated
- grad_gain_one: float32 [1024], replicated
- grad_shift_one: float32 [1024], replicated
- grad_w_hidden: float32 [1024, 4096], P(('shard', 'ctx'), 'tensor')
- grad_b_hidden: float32 [4096], P('tensor')
- grad_w_down: float32 [1024, 4096], P(('shard', 'ctx'), 'tensor')
- grad_b_down: float32 [1024], replicated
- grad_gain_two: float32 [1024], replicated
- grad_shift_two: float32 [1024], replicated
Inputs may be any that keep to these rules, and one draw needn't show every extreme that they name: `valid_mask`: 0 or 1; the last token of every sequence is valid.
All inputs are finite; a program needn't handle non-finite values.
Results may differ from a plain program's by a relative error of at most 0.018.
Values may be sent and summed in bfloat16 or wider, within the bound.
No kernel may reach another device: no remote copies, remote signals or barrier semaphores. Data moves between devices by JAX's collectives and lax.ppermute only.
A program may use at most 256 MiB of HBM per device.

v0:
```python
from functools import partial
import math
import jax
import jax.numpy as jnp
from jax import lax
from jax.sharding import PartitionSpec as P

D = 1024
HEADS = 16


def layer_norm(value, gain, shift):
    center = jnp.mean(value, axis=-1, keepdims=True)
    offset = value - center
    spread = jnp.mean(offset * offset, axis=-1, keepdims=True)
    return offset * lax.rsqrt(spread + 1e-05) * gain + shift


def contract(left, right, left_dim, right_dim):
    return lax.dot_general(
        left, right, (((left_dim,), (right_dim,)), ((), ())), preferred_element_type=jnp.float32
    )


def block_rows(length):
    return math.gcd(length, 512)


def score_block(queries, keys, scale):
    return jnp.einsum("qshd,kshd->qshk", queries, keys, preferred_element_type=jnp.float32) * scale


def fold_block(carry, keys, values, queries, scale):
    peak, total, summed = carry
    scores = score_block(queries, keys, scale)
    new_peak = jnp.maximum(peak, jnp.max(scores, axis=-1))
    fade = jnp.exp(peak - new_peak)
    weights = jnp.exp(scores - new_peak[..., None])
    total = total * fade + jnp.sum(weights, axis=-1)
    summed = summed * fade[..., None] + jnp.einsum(
        "qshk,kshd->qshd", weights.astype(jnp.bfloat16), values, preferred_element_type=jnp.float32
    )
    return (new_peak, total, summed)


def fold_keys(carry, piece, start, queries, scale):
    keys, values = piece
    length, seqs, width = keys.shape
    heads = queries.shape[2]
    head_size = width // heads
    block = block_rows(length)
    blocks = length // block
    keys = keys.reshape(blocks, block, seqs, heads, head_size)
    values = values.reshape(blocks, block, seqs, heads, head_size)

    def step(inner, pair):
        return (fold_block(inner, pair[0], pair[1], queries, scale), None)

    carry, unused = lax.scan(step, carry, (keys, values))
    return carry


def score_grads(keys, values, queries, out_grad, logsum, delta, scale):
    scores = score_block(queries, keys, scale)
    weights = jnp.exp(scores - logsum[..., None])
    weight_grad = jnp.einsum(
        "qshd,kshd->qshk", out_grad, values, preferred_element_type=jnp.float32
    )
    score_grad = (weights * (weight_grad - delta[..., None])).astype(jnp.bfloat16)
    return (weights, score_grad)


def pair_grads(keys, values, queries, out_grad, logsum, delta, scale):
    block, seqs = (keys.shape[0], keys.shape[1])
    weights, score_grad = score_grads(keys, values, queries, out_grad, logsum, delta, scale)
    value_grad = jnp.einsum(
        "qshk,qshd->kshd",
        weights.astype(jnp.bfloat16),
        out_grad,
        preferred_element_type=jnp.float32,
    )
    key_grad = (
        jnp.einsum("qshk,qshd->kshd", score_grad, queries, preferred_element_type=jnp.float32)
        * scale
    )
    joined = jnp.concatenate(
        [key_grad.reshape(block, seqs, -1), value_grad.reshape(block, seqs, -1)], axis=-1
    )
    return (score_grad, joined)


def back_block(query_grad, pair, queries, out_grad, logsum, delta, scale):
    keys, values = pair
    score_grad, joined = pair_grads(keys, values, queries, out_grad, logsum, delta, scale)
    query_grad = (
        query_grad
        + jnp.einsum("qshk,kshd->qshd", score_grad, keys, preferred_element_type=jnp.float32)
        * scale
    )
    return (query_grad, joined)


def body(
    inputs,
    time_features,
    valid_mask,
    teacher,
    w_time,
    b_time,
    w_query,
    b_query,
    w_key,
    w_value,
    b_value,
    w_output,
    b_output,
    gain_one,
    shift_one,
    w_hidden,
    b_hidden,
    w_down,
    b_down,
    gain_two,
    shift_two,
):
    positions, seqs, width = inputs.shape
    rows_local = positions * seqs
    head_size = D // HEADS
    scale = 1.0 / math.sqrt(head_size)
    embed = jnp.dot(time_features, w_time, preferred_element_type=jnp.float32) + b_time
    start = (inputs.astype(jnp.float32) + embed[None]).reshape(rows_local, width)
    start_low = start.astype(jnp.bfloat16)
    full_query, full_key, full_value, full_output = (
        lax.all_gather(w_query, "shard", axis=0, tiled=True),
        lax.all_gather(w_key, "shard", axis=0, tiled=True),
        lax.all_gather(w_value, "shard", axis=0, tiled=True),
        lax.all_gather(w_output, "shard", axis=0, tiled=True),
    )
    columns = full_query.shape[1]
    heads = columns // head_size
    query_low = (
        jnp.dot(start_low, full_query, preferred_element_type=jnp.float32) + b_query
    ).astype(jnp.bfloat16)
    key_low = jnp.dot(start_low, full_key, preferred_element_type=jnp.float32).astype(jnp.bfloat16)
    value_low = (
        jnp.dot(start_low, full_value, preferred_element_type=jnp.float32) + b_value
    ).astype(jnp.bfloat16)
    queries = query_low.reshape(positions, seqs, heads, head_size)
    key_local = key_low.reshape(positions, seqs, columns)
    value_local = value_low.reshape(positions, seqs, columns)
    initial = (
        jnp.full((positions, seqs, heads), -1e30, jnp.float32),
        jnp.zeros((positions, seqs, heads), jnp.float32),
        jnp.zeros((positions, seqs, heads, head_size), jnp.float32),
    )
    folder = partial(fold_keys, queries=queries, scale=scale)
    peak, total, summed = folder(
        initial,
        (
            lax.all_gather(key_local, "ctx", axis=0, tiled=True),
            lax.all_gather(value_local, "ctx", axis=0, tiled=True),
        ),
        jnp.int32(0),
    )
    attended = summed / total[..., None]
    logsum = peak + jnp.log(total)
    mixed_low = attended.reshape(rows_local, columns).astype(jnp.bfloat16)
    branch_part = contract(mixed_low, full_output, 1, 1)
    branch = lax.psum(branch_part.astype(jnp.bfloat16), "tensor").astype(jnp.float32) + b_output
    normed, norm_back_one = jax.vjp(layer_norm, start + branch, gain_one, shift_one)
    normed_low = normed.astype(jnp.bfloat16)
    full_hidden, full_down = (
        lax.all_gather(w_hidden, "shard", axis=0, tiled=True),
        lax.all_gather(w_down, "shard", axis=0, tiled=True),
    )
    pre_act = jnp.dot(normed_low, full_hidden, preferred_element_type=jnp.float32) + b_hidden
    hidden, gelu_back = jax.vjp(partial(jax.nn.gelu, approximate=False), pre_act)
    hidden_low = hidden.astype(jnp.bfloat16)
    feed_part = contract(hidden_low, full_down, 1, 1)
    feed = lax.psum(feed_part.astype(jnp.bfloat16), "tensor").astype(jnp.float32) + b_down
    result, norm_back_two = jax.vjp(layer_norm, normed + feed, gain_two, shift_two)
    layer_out = result.astype(jnp.bfloat16).reshape(positions, seqs, width)
    valid = valid_mask.astype(jnp.float32).reshape(rows_local)
    error = result - teacher.reshape(rows_local, width).astype(jnp.float32)
    squares_local = jnp.sum(valid[:, None] * error * error)
    squares_total, count = lax.psum((squares_local, jnp.sum(valid)), ("shard", "ctx"))
    loss = squares_total / (D * count)
    tokens_all = rows_local * lax.axis_size("ctx") * lax.axis_size("shard")
    result_grad = 2.0 * tokens_all / count * valid[:, None] * error
    sum_grad, grad_gain_two, grad_shift_two = norm_back_two(result_grad)
    feed_low = sum_grad.astype(jnp.bfloat16)
    grad_down = contract(feed_low, hidden_low, 0, 0)
    hidden_grad = jnp.dot(feed_low, full_down, preferred_element_type=jnp.float32)
    pre_grad = gelu_back(hidden_grad)[0].astype(jnp.bfloat16)
    grad_hidden = contract(normed_low, pre_grad, 0, 0)
    normed_part = contract(pre_grad, full_hidden, 1, 1)
    normed_grad = sum_grad + lax.psum(normed_part.astype(jnp.bfloat16), "tensor").astype(
        jnp.float32
    )
    first_grad, grad_gain_one, grad_shift_one = norm_back_one(normed_grad)
    branch_low = first_grad.astype(jnp.bfloat16)
    grad_output = contract(branch_low, mixed_low, 0, 0)
    mixed_grad = jnp.dot(branch_low, full_output, preferred_element_type=jnp.float32).astype(
        jnp.bfloat16
    )
    out_grad = mixed_grad.reshape(positions, seqs, heads, head_size)
    delta = jnp.sum(out_grad.astype(jnp.float32) * attended, axis=-1)
    all_keys, all_values = (
        lax.all_gather(key_local, "ctx", axis=0, tiled=True),
        lax.all_gather(value_local, "ctx", axis=0, tiled=True),
    )
    length = all_keys.shape[0]
    block = block_rows(length)
    key_blocks = all_keys.reshape(length // block, block, seqs, heads, head_size)
    value_blocks = all_values.reshape(length // block, block, seqs, heads, head_size)
    query_zero = jnp.zeros((positions, seqs, heads, head_size), jnp.float32)
    back_step = partial(
        back_block, queries=queries, out_grad=out_grad, logsum=logsum, delta=delta, scale=scale
    )
    query_grad, joined = lax.scan(back_step, query_zero, (key_blocks, value_blocks))
    joined = joined.reshape(length, seqs, 2 * columns)
    owned = lax.psum_scatter(
        joined.astype(jnp.bfloat16), "ctx", scatter_dimension=0, tiled=True
    ).astype(jnp.float32)
    key_grad_low = owned[:, :, :columns].reshape(rows_local, columns).astype(jnp.bfloat16)
    value_grad_low = owned[:, :, columns:].reshape(rows_local, columns).astype(jnp.bfloat16)
    query_grad_low = query_grad.reshape(rows_local, columns).astype(jnp.bfloat16)
    grad_query = contract(start_low, query_grad_low, 0, 0)
    grad_key = contract(start_low, key_grad_low, 0, 0)
    grad_value = contract(start_low, value_grad_low, 0, 0)
    start_part = (
        contract(query_grad_low, full_query, 1, 1)
        + contract(key_grad_low, full_key, 1, 1)
        + contract(value_grad_low, full_value, 1, 1)
    )
    start_grad = first_grad + lax.psum(start_part.astype(jnp.bfloat16), "tensor").astype(
        jnp.float32
    )
    grad_inputs = start_grad.reshape(positions, seqs, width)
    embed_grad = jnp.sum(grad_inputs, axis=0)
    time_grad = jnp.dot(
        time_features.astype(jnp.float32).T, embed_grad, precision=lax.Precision.HIGHEST
    )
    (
        grad_w_time,
        grad_b_time,
        grad_b_query,
        grad_b_value,
        grad_b_output,
        grad_gain_one,
        grad_shift_one,
        grad_b_hidden,
        grad_b_down,
        grad_gain_two,
        grad_shift_two,
    ) = lax.psum(
        (
            time_grad,
            jnp.sum(embed_grad, axis=0),
            jnp.sum(query_grad_low.astype(jnp.float32), axis=0),
            jnp.sum(value_grad_low.astype(jnp.float32), axis=0),
            jnp.sum(branch_low.astype(jnp.float32), axis=0),
            grad_gain_one,
            grad_shift_one,
            jnp.sum(pre_grad.astype(jnp.float32), axis=0),
            jnp.sum(feed_low.astype(jnp.float32), axis=0),
            grad_gain_two,
            grad_shift_two,
        ),
        ("shard", "ctx"),
    )
    grad_w_query, grad_w_key, grad_w_value, grad_w_output, grad_w_hidden, grad_w_down = (
        lax.psum_scatter(grad_query, ("shard", "ctx"), scatter_dimension=0, tiled=True),
        lax.psum_scatter(grad_key, ("shard", "ctx"), scatter_dimension=0, tiled=True),
        lax.psum_scatter(grad_value, ("shard", "ctx"), scatter_dimension=0, tiled=True),
        lax.psum_scatter(grad_output, ("shard", "ctx"), scatter_dimension=0, tiled=True),
        lax.psum_scatter(grad_hidden, ("shard", "ctx"), scatter_dimension=0, tiled=True),
        lax.psum_scatter(grad_down, ("shard", "ctx"), scatter_dimension=0, tiled=True),
    )
    return (
        layer_out,
        loss,
        grad_inputs,
        grad_w_time,
        grad_b_time,
        grad_w_query,
        grad_b_query,
        grad_w_key,
        grad_w_value,
        grad_b_value,
        grad_w_output,
        grad_b_output,
        grad_gain_one,
        grad_shift_one,
        grad_w_hidden,
        grad_b_hidden,
        grad_w_down,
        grad_b_down,
        grad_gain_two,
        grad_shift_two,
    )


def solution(mesh):
    placed = (
        P("ctx", "shard", None),
        P("shard", None),
        P("ctx", "shard"),
        P("ctx", "shard", None),
        P(),
        P(),
        P("shard", "tensor"),
        P("tensor"),
        P("shard", "tensor"),
        P("shard", "tensor"),
        P("tensor"),
        P("shard", "tensor"),
        P(),
        P(),
        P(),
        P("shard", "tensor"),
        P("tensor"),
        P("shard", "tensor"),
        P(),
        P(),
        P(),
    )
    return jax.shard_map(
        body,
        mesh=mesh,
        in_specs=placed,
        out_specs=(
            P("ctx", "shard", None),
            P(),
            P("ctx", "shard", None),
            P(),
            P(),
            P(("shard", "ctx"), "tensor"),
            P("tensor"),
            P(("shard", "ctx"), "tensor"),
            P(("shard", "ctx"), "tensor"),
            P("tensor"),
            P(("shard", "ctx"), "tensor"),
            P(),
            P(),
            P(),
            P(("shard", "ctx"), "tensor"),
            P("tensor"),
            P(("shard", "ctx"), "tensor"),
            P(),
            P(),
            P(),
        ),
        check_vma=False,
    )
```

profile of v0, /device:TPU:0, one launch (start us, length us, event | category | flops | bytes accessed | tf_op | source)
XLA Modules:
  0.0 1141.1 jit_solution(9354903953610810085)
XLA Ops:
  10.0 5.7 fusion.56
  15.6 5.3 reshape.180
  21.0 10.0 all_gather.26
  35.5 8.2 all_gather.29
  48.8 7.4 all_gather.28
  60.6 7.3 all_gather.31
  67.9 15.4 %all-gather.5.cloned.1.call-done = bf16[1024,4,256]{0,2,1:T(8,128)(2,1)} async-done(((bf16[256,4,256]{0,2,1:T(8,128)(2,1)}), bf16[1024,4,256]{0,2,1:T(8,128)(2,1)}) %all-gather.5.cloned.1.call-update) | async-done | bytes 2097168 | tf_op jit(solution)/shard_map/all_gather | solution.py:160
  89.8 40.1 %all-gather.7.cloned.1.call-done = bf16[1024,4,256]{0,2,1:T(8,128)(2,1)} async-done(((bf16[256,4,256]{0,2,1:T(8,128)(2,1)}), bf16[1024,4,256]{0,2,1:T(8,128)(2,1)}) %all-gather.7.cloned.1.call-update) | async-done | bytes 2097168 | tf_op jit(solution)/shard_map/all_gather | solution.py:161
  137.8 28.7 %while.28 = (s32[]{:T(128)}, f32[256,4,4]{0,2,1:T(4,128)S(1)}, f32[256,4,4]{0,2,1:T(4,128)S(1)}, f32[256,4,4,64]{0,3,2,1:T(8,128)}, bf16[2,512,4,4,64]{1,4,3,2,0...) while((s32[]{:T(128)}, f32[256,4,4]{0,2,1:T(4,128)S(1)}, ...), condition=%wide.region_3.4_spmd.clone, body=%wide.region_0.3_spmd.clone.sunk | while | flops 554455040 | bytes 63701640 | solution.py:59
  180.3 48.4 %all-reduce.7.cloned.1.call-done = bf16[1024,1024]{1,0:T(8,128)(2,1)} async-done(((bf16[1024,1024]{1,0:T(8,128)(2,1)}), bf16[1024,1024]{1,0:T(8,128)(2,1)}) %all-reduce.7.cloned.1.call-update) | async-done | bytes 2097168 | tf_op jit(solution)/shard_map/psum | solution.py:169
  234.7 15.7 %multiply_convert_fusion = (bf16[1024,1024]{1,0:T(8,128)(2,1)}, f32[1024,1024]{1,0:T(8,128)}, f32[1024,1024]{1,0:T(8,128)}) fusion(f32[1024]{0:T(1024)S(1)} %copy-done.47, bf16[1024,1024]{1,0:T(8,128)(2,1)} %all-gather.9.cloned.1.call-done, f32[1024,1024]{1,0:T(8,128)} %copy-done.4, f32[1024]{0:T(1024)S(1)} %copy-done.42, f32[1024]{0:T(1024)S(1)} %copy-done.32, ...), kind=kOutput, calls=%fused_computation.69 | convolution fusion | flops 2221932544 | bytes 16797696 | tf_op jit(solution)/shard_map/dot_general | solution.py:176
  250.4 5.9 convolution_convert_fusion.1
  257.0 22.5 %psum.122 = f32[]{:T(128)} all-reduce(f32[]{:T(128)} %convert_reduce_fusion.5), channel_id=1, replica_groups=mesh['shard'=2,'ctx'=4,'tensor'=4] {'shard','ctx'}, use_global_device_ids=true, to_apply=%region_13.14 | all-reduce | flops 1 | bytes 8 | tf_op jit(solution)/shard_map/psum | solution.py:186
  284.8 23.2 %all-reduce.9.cloned.1.call-done = bf16[1024,1024]{1,0:T(8,128)(2,1)} async-done(((bf16[1024,1024]{1,0:T(8,128)(2,1)}), bf16[1024,1024]{1,0:T(8,128)(2,1)}) %all-reduce.9.cloned.1.call-update) | async-done | bytes 2097168 | tf_op jit(solution)/shard_map/psum | solution.py:180
  313.9 5.5 multiply_reduce_fusion
  335.4 51.3 %all-reduce.11.cloned.1.call-done = bf16[1024,1024]{1,0:T(8,128)(2,1)} async-done(((bf16[1024,1024]{1,0:T(8,128)(2,1)}), bf16[1024,1024]{1,0:T(8,128)(2,1)}) %all-reduce.11.cloned.1.call-update) | async-done | bytes 2097168 | tf_op jit(solution)/shard_map/psum | solution.py:197
  404.0 7.8 multiply_reduce_fusion.7
  414.7 25.0 %while.29 = (s32[]{:T(128)}, f32[256,4,4,64]{0,3,2,1:T(8,128)}, bf16[2,512,4,512]{1,3,2,0:T(8,128)(2,1)}, bf16[2,512,4,4,64]{1,4,3,2,0:T(8,128)(2,1)S(1)}, bf16[...) while((s32[]{:T(128)}, f32[256,4,4,64]{0,3,2,1:T(8,128)}, ...), condition=%wide.region_21.22_spmd.clone, body=%wide.region_20.21_spmd.clone.sunk | while | flops 1364983808 | bytes 76595896 | solution.py:220
  439.7 7.3 copy.94
  452.8 71.2 %reduce-scatter.8.cloned.1.call-done = bf16[256,4,512]{2,0,1:T(8,128)(2,1)} async-done(((bf16[1024,4,512]{2,0,1:T(8,128)(2,1)}), bf16[256,4,512]{2,0,1:T(8,128)(2,1)}) %reduce-scatter.8.cloned.1.call-update) | async-done | bytes 1048592 | tf_op jit(solution)/shard_map/reduce_scatter | solution.py:222
  530.0 5.5 add_convert_fusion
  535.6 52.0 %all-reduce.13.cloned.1.call-done = bf16[1024,1024]{1,0:T(8,128)(2,1)} async-done(((bf16[1024,1024]{1,0:T(8,128)(2,1)}), bf16[1024,1024]{1,0:T(8,128)(2,1)}) %all-reduce.13.cloned.1.call-update) | async-done | bytes 2097168 | tf_op jit(solution)/shard_map/psum | solution.py:236
  587.6 5.4 fusion.68
  611.7 7.5 fusion.63
  619.5 6.6 fusion.80
  638.8 38.8 %all-reduce = (f32[]{:T(128)}, f32[1024]{0:T(1024)}, f32[256]{0:T(256)}, f32[256]{0:T(256)}, f32[1024]{0:T(1024)}, /*index=5*/f32[1024]{0:T(1024)}, f32[1024]{0:...) all-reduce(f32[]{:T(128)} %get-tuple-element.280, ...), channel_id=1, replica_groups=mesh['shard'=2,'ctx'=4,'tensor'=4] {'shard','ctx'}, use_global_device_ids=true, to_apply=%region_11.12 | all-reduce | flops 8705 | bytes 69640 | tf_op jit(solution)/shard_map/psum | solution.py:186
  683.5 64.4 %reduce-scatter.16.cloned.1.call-done = f32[128,256]{1,0:T(8,128)} async-done(((f32[1024,256]{1,0:T(8,128)}), f32[128,256]{1,0:T(8,128)}) %reduce-scatter.16.cloned.1.call-update) | async-done | bytes 131088 | tf_op jit(solution)/shard_map/reduce_scatter | solution.py:276
  747.9 67.0 %reduce-scatter.10.cloned.1.call-done = f32[128,256]{1,0:T(8,128)} async-done(((f32[1024,256]{1,0:T(8,128)}), f32[128,256]{1,0:T(8,128)}) %reduce-scatter.10.cloned.1.call-update) | async-done | bytes 131088 | tf_op jit(solution)/shard_map/reduce_scatter | solution.py:273
  815.0 91.1 %reduce-scatter.18.cloned.1.call-done = f32[128,1024]{1,0:T(8,128)} async-done(((f32[1024,1024]{1,0:T(8,128)}), f32[128,1024]{1,0:T(8,128)}) %reduce-scatter.18.cloned.1.call-update) | async-done | bytes 524304 | tf_op jit(solution)/shard_map/reduce_scatter | solution.py:277
  906.1 92.1 %reduce-scatter.20.cloned.1.call-done = f32[128,1024]{1,0:T(8,128)} async-done(((f32[1024,1024]{1,0:T(8,128)}), f32[128,1024]{1,0:T(8,128)}) %reduce-scatter.20.cloned.1.call-update) | async-done | bytes 524304 | tf_op jit(solution)/shard_map/reduce_scatter | solution.py:278
  998.2 67.1 %reduce-scatter.14.cloned.1.call-done = f32[128,256]{1,0:T(8,128)} async-done(((f32[1024,256]{1,0:T(8,128)}), f32[128,256]{1,0:T(8,128)}) %reduce-scatter.14.cloned.1.call-update) | async-done | bytes 131088 | tf_op jit(solution)/shard_map/reduce_scatter | solution.py:275
  1065.3 66.8 %reduce-scatter.12.cloned.1.call-done = f32[128,256]{1,0:T(8,128)} async-done(((f32[1024,256]{1,0:T(8,128)}), f32[128,256]{1,0:T(8,128)}) %reduce-scatter.12.cloned.1.call-update) | async-done | bytes 131088 | tf_op jit(solution)/shard_map/reduce_scatter | solution.py:274
  (244 shorter events, 198.4 us)
Async XLA Ops:
  8.0 75.3 %all-gather.5.cloned.1.call-start = ((), (), s32[]{:S(2)}) async-start(), calls=%async_computation.7 | async-start | bytes 2621440 | tf_op jit(solution)/shard_map/all_gather | solution.py:160
  21.0 14.5 %copy-start.29 = (bf16[512,256]{1,0:T(8,128)(2,1)S(1)}, bf16[512,256]{1,0:T(8,128)(2,1)}, u32[]{:S(2)}) copy-start(bf16[512,256]{1,0:T(8,128)(2,1)} %param.34) | copy-start | bytes 786436
  31.0 12.6 %copy-start.15 = (bf16[1024,256]{1,0:T(8,128)(2,1)}, bf16[1024,256]{1,0:T(8,128)(2,1)S(1)}, u32[]{:S(2)}) copy-start(bf16[1024,256]{1,0:T(8,128)(2,1)S(1)} %all_gather.26) | copy-start | bytes 1572868
  31.0 13.4 %copy-start.43 = (f32[256]{0:T(256)S(1)}, f32[256]{0:T(256)}, u32[]{:S(2)}) copy-start(f32[256]{0:T(256)} %param.35) | copy-start | bytes 3076
  35.4 13.4 %copy-start.30 = (bf16[512,256]{1,0:T(8,128)(2,1)S(1)}, bf16[512,256]{1,0:T(8,128)(2,1)}, u32[]{:S(2)}) copy-start(bf16[512,256]{1,0:T(8,128)(2,1)} %param.31) | copy-start | bytes 786436
  35.4 94.5 %all-gather.7.cloned.1.call-start = ((), (), s32[]{:S(2)}) async-start(), calls=%async_computation.8 | async-start | bytes 2621440 | tf_op jit(solution)/shard_map/all_gather | solution.py:161
  44.4 11.8 %copy-start.44 = (f32[256]{0:T(256)S(1)}, f32[256]{0:T(256)}, u32[]{:S(2)}) copy-start(f32[256]{0:T(256)} %param.32) | copy-start | bytes 3076
  48.7 179.9 %all-reduce.7.cloned.1.call-start = ((), (), s32[]{:S(2)}) async-start(), calls=%async_computation.9 | async-start | bytes 4194304 | tf_op jit(solution)/shard_map/psum | solution.py:169
  172.8 55.9 %copy-start.39 = (f32[1024]{0:T(1024)S(1)}, f32[1024]{0:T(1024)}, u32[]{:S(2)}) copy-start(f32[1024]{0:T(1024)} %param.37) | copy-start | bytes 12292
  178.9 55.8 %all-gather.9.cloned.1.call-start = ((), (), s32[]{:S(2)}) async-start(), calls=%async_computation.10 | async-start | bytes 3145728 | tf_op jit(solution)/shard_map/all_gather | solution.py:173
  179.4 71.0 %all-gather.11.cloned.1.call-start = ((), (), s32[]{:S(2)}) async-start(), calls=%async_computation.11 | async-start | bytes 3145728 | tf_op jit(solution)/shard_map/all_gather | solution.py:174
  180.0 128.0 %all-reduce.9.cloned.1.call-start = ((), (), s32[]{:S(2)}) async-start(), calls=%async_computation.12 | async-start | bytes 4194304 | tf_op jit(solution)/shard_map/psum | solution.py:180
  256.4 51.6 %copy-start.40 = (f32[1024]{0:T(1024)S(1)}, f32[1024]{0:T(1024)}, u32[]{:S(2)}) copy-start(f32[1024]{0:T(1024)} %param.43) | copy-start | bytes 12292
  256.4 130.4 %all-reduce.11.cloned.1.call-start = ((), (), s32[]{:S(2)}) async-start(), calls=%async_computation.13 | async-start | bytes 4194304 | tf_op jit(solution)/shard_map/psum | solution.py:197
  321.4 8.7 copy-start.7
  322.4 7.7 copy-start.23
  335.2 188.8 %reduce-scatter.8.cloned.1.call-start = ((), (), s32[]{:S(2)}) async-start(), calls=%async_computation.14 | async-start | bytes 5242880 | tf_op jit(solution)/shard_map/reduce_scatter | solution.py:222
  386.8 6.5 copy-start.8
  386.8 7.1 copy-start.14
  447.0 140.6 %all-reduce.13.cloned.1.call-start = ((), (), s32[]{:S(2)}) async-start(), calls=%async_computation.15 | async-start | bytes 4194304 | tf_op jit(solution)/shard_map/psum | solution.py:236
  450.1 75.7 %copy-start.16 = (bf16[1024,256]{1,0:T(8,128)(2,1)S(1)}, bf16[1024,256]{1,0:T(8,128)(2,1)}, u32[]{:S(2)}) copy-start(bf16[1024,256]{1,0:T(8,128)(2,1)} %copy-done.15) | copy-start | bytes 1572868
  535.5 145.5 %all-reduce.15.cloned.1.call-start = ((), (), s32[]{:S(2)}) async-start(), calls=%async_computation.16 | async-start | bytes 2097152 | tf_op jit(solution)/shard_map/psum | solution.py:256
  602.7 145.2 %reduce-scatter.16.cloned.1.call-start = ((), (), s32[]{:S(2)}) async-start(), calls=%async_computation.20 | async-start | bytes 1179648 | tf_op jit(solution)/shard_map/reduce_scatter | solution.py:276
  606.1 208.8 %reduce-scatter.10.cloned.1.call-start = ((), (), s32[]{:S(2)}) async-start(), calls=%async_computation.17 | async-start | bytes 1179648 | tf_op jit(solution)/shard_map/reduce_scatter | solution.py:273
  611.6 294.5 %reduce-scatter.18.cloned.1.call-start = ((), (), s32[]{:S(2)}) async-start(), calls=%async_computation.21 | async-start | bytes 4718592 | tf_op jit(solution)/shard_map/reduce_scatter | solution.py:277
  619.2 379.0 %reduce-scatter.20.cloned.1.call-start = ((), (), s32[]{:S(2)}) async-start(), calls=%async_computation.22 | async-start | bytes 4718592 | tf_op jit(solution)/shard_map/reduce_scatter | solution.py:278
  626.0 439.2 %reduce-scatter.14.cloned.1.call-start = ((), (), s32[]{:S(2)}) async-start(), calls=%async_computation.19 | async-start | bytes 1179648 | tf_op jit(solution)/shard_map/reduce_scatter | solution.py:275
  632.2 6.6 copy-start.34
  632.2 6.6 copy-start.35
  632.2 6.6 copy-start.36
  632.2 499.9 %reduce-scatter.12.cloned.1.call-start = ((), (), s32[]{:S(2)}) async-start(), calls=%async_computation.18 | async-start | bytes 1179648 | tf_op jit(solution)/shard_map/reduce_scatter | solution.py:274
  632.3 499.8 %copy-start.1 = (bf16[256,1024]{1,0:T(8,128)(2,1)S(1)}, bf16[256,1024]{1,0:T(8,128)(2,1)}, u32[]{:S(2)}) copy-start(bf16[256,1024]{1,0:T(8,128)(2,1)} %param.29) | copy-start | bytes 1572868
  (38 other events, 120.6 us)
Sparse Core Ops, SparseCore 0:
  35.5 47.7 all-gather.4
  85.5 44.4 all-gather.6
  179.0 49.6 all-reduce.6
  256.5 51.4 all-reduce.8
  335.3 51.4 all-reduce.10
  447.2 76.8 reduce-scatter.7
  535.7 51.9 all-reduce.12
Sparse Core Ops, SparseCore 1:
  180.9 31.2 all-gather.8
  213.7 33.0 all-gather.10
  602.8 78.2 all-reduce.14
  685.0 62.9 reduce-scatter.15
  752.3 62.6 reduce-scatter.9
  819.2 86.9 reduce-scatter.17
  910.6 87.5 reduce-scatter.19
  1002.0 63.2 reduce-scatter.13
  1069.5 62.5 reduce-scatter.11
where the time goes:
time: 1150 us; the launch traced here: 1140 us
  waiting for transfers between devices  754 us (66%)
  matrix products  123 us (11%)
  blocking collectives  94.3 us (8%)
  local copies, waits for them, and re-layouts  85 us (7%)
  other arithmetic  63.5 us (6%)
  between operations  19.9 us (2%)
    reduce_scatter x1, waiting for transfers between devices, body(): lax.psum_scatter(grad_down, ('shard', 'ctx'), scatter_dimension=0, tiled=...  92.1 us
    reduce_scatter x1, waiting for transfers between devices, body(): lax.psum_scatter(grad_hidden, ('shard', 'ctx'), scatter_dimension=0, tile...  91.1 us
    reduce_scatter x1, waiting for transfers between devices, body(): lax.psum_scatter(joined.astype(jnp.bfloat16), 'ctx', scatter_dimension=0,...  71.2 us
    reduce_scatter x1, waiting for transfers between devices, body(): lax.psum_scatter(grad_value, ('shard', 'ctx'), scatter_dimension=0, tiled...  67.1 us
    reduce_scatter x1, waiting for transfers between devices, body(): lax.psum_scatter(grad_query, ('shard', 'ctx'), scatter_dimension=0, tiled...  67 us
    reduce_scatter x1, waiting for transfers between devices, body(): lax.psum_scatter(grad_key, ('shard', 'ctx'), scatter_dimension=0, tiled=T...  66.8 us
    reduce_scatter x1, waiting for transfers between devices, body(): lax.psum_scatter(grad_output, ('shard', 'ctx'), scatter_dimension=0, tile...  64.4 us
    psum x2, blocking collectives, body(): lax.psum((squares_local, jnp.sum(valid)), ('shard', 'ctx'))  61.4 us
  transfers between devices with their start and end apart: 16, of which 14 were waited for; matrix products, arithmetic and copies ran while one was open for 7% of the time, Pallas kernels for 0%

commit v1 on v0

--- a/solution.py
+++ b/solution.py
@@ -166,7 +166,10 @@
     logsum = peak + jnp.log(total)
     mixed_low = attended.reshape(rows_local, columns).astype(jnp.bfloat16)
     branch_part = contract(mixed_low, full_output, 1, 1)
-    branch = lax.psum(branch_part.astype(jnp.bfloat16), "tensor").astype(jnp.float32) + b_output
+    branch = (
+        lax.all_gather(branch_part.astype(jnp.bfloat16), "tensor").sum(axis=0).astype(jnp.float32)
+        + b_output
+    )
     normed, norm_back_one = jax.vjp(layer_norm, start + branch, gain_one, shift_one)
     normed_low = normed.astype(jnp.bfloat16)
     full_hidden, full_down = (

time: 1150 us -> 1200 us (1.043)
  waiting for transfers between devices: 754 us -> 790 us
  other arithmetic: 63.5 us -> 78.1 us
    all_gather x0 -> x1, waiting for transfers between devices: none -> 55.5 us  [body(): lax.all_gather(branch_part.astype(jnp.bfloat16), 'tensor').sum(axis=0)]
    psum x1 -> x0, waiting for transfers between devices: 48.4 us -> none  [body(): lax.psum(branch_part.astype(jnp.bfloat16), 'tensor').astype(jnp.float32)]
    all_gather x1, waiting for transfers between devices: 0.01 us -> 19 us  [body(): lax.all_gather(w_down, 'shard', axis=0, tiled=True)]
    unnamed x102 -> x105, local copies, waits for them, and re-layouts: 29.2 us -> 27.2 us
  transfers between devices with their start and end apart: 16 -> 16, of which waited for: 14 -> 16; matrix products, arithmetic and copies ran while one was open for 7% -> 9% of each run, Pallas kernels for 0% -> 0%
where the time goes in v1:
time: 1200 us; the launch traced here: 1190 us
  waiting for transfers between devices  790 us (66%)
  matrix products  122 us (10%)
  blocking collectives  93.2 us (8%)
  local copies, waits for them, and re-layouts  89 us (7%)
  other arithmetic  78.1 us (7%)
  between operations  17.9 us (1%)
    reduce_scatter x1, waiting for transfers between devices, body(): lax.psum_scatter(grad_down, ('shard', 'ctx'), scatter_dimension=0, tiled=...  91.8 us
    reduce_scatter x1, waiting for transfers between devices, body(): lax.psum_scatter(grad_hidden, ('shard', 'ctx'), scatter_dimension=0, tile...  91.6 us
    reduce_scatter x1, waiting for transfers between devices, body(): lax.psum_scatter(joined.astype(jnp.bfloat16), 'ctx', scatter_dimension=0,...  70.8 us
    reduce_scatter x1, waiting for transfers between devices, body(): lax.psum_scatter(grad_value, ('shard', 'ctx'), scatter_dimension=0, tiled...  67.3 us
    reduce_scatter x1, waiting for transfers between devices, body(): lax.psum_scatter(grad_key, ('shard', 'ctx'), scatter_dimension=0, tiled=T...  66.4 us
    reduce_scatter x1, waiting for transfers between devices, body(): lax.psum_scatter(grad_output, ('shard', 'ctx'), scatter_dimension=0, tile...  66.4 us
    reduce_scatter x1, waiting for transfers between devices, body(): lax.psum_scatter(grad_query, ('shard', 'ctx'), scatter_dimension=0, tiled...  64.8 us
    psum x2, blocking collectives, body(): lax.psum((squares_local, jnp.sum(valid)), ('shard', 'ctx'))  60.1 us
  transfers between devices with their start and end apart: 16, of which 16 were waited for; matrix products, arithmetic and copies ran while one was open for 9% of the time, Pallas kernels for 0%

profile of v1, /device:TPU:0, one launch (start us, length us, event | category | flops | bytes accessed | tf_op | source)
XLA Modules:
  0.0 1191.6 jit_solution(6065568280686438069)
XLA Ops:
  18.7 10.0 all_gather.32
  33.2 8.2 all_gather.35
  46.5 7.4 all_gather.34
  58.3 7.4 all_gather.37
  65.8 15.2 %all-gather.7.cloned.1.call-done = bf16[1024,4,256]{0,2,1:T(8,128)(2,1)} async-done(((bf16[256,4,256]{0,2,1:T(8,128)(2,1)}), bf16[1024,4,256]{0,2,1:T(8,128)(2,1)}) %all-gather.7.cloned.1.call-update) | async-done | bytes 2097168 | tf_op jit(solution)/shard_map/all_gather | solution.py:160
  87.5 40.1 %all-gather.9.cloned.1.call-done = bf16[1024,4,256]{0,2,1:T(8,128)(2,1)} async-done(((bf16[256,4,256]{0,2,1:T(8,128)(2,1)}), bf16[1024,4,256]{0,2,1:T(8,128)(2,1)}) %all-gather.9.cloned.1.call-update) | async-done | bytes 2097168 | tf_op jit(solution)/shard_map/all_gather | solution.py:161
  135.5 28.7 %while.28 = (s32[]{:T(128)}, f32[256,4,4]{0,2,1:T(4,128)S(1)}, f32[256,4,4]{0,2,1:T(4,128)S(1)}, f32[256,4,4,64]{0,3,2,1:T(8,128)}, bf16[2,512,4,4,64]{1,4,3,2,0...) while((s32[]{:T(128)}, f32[256,4,4]{0,2,1:T(4,128)S(1)}, ...), condition=%wide.region_3.4_spmd.clone, body=%wide.region_0.3_spmd.clone.sunk | while | flops 554455040 | bytes 63701640 | solution.py:59
  177.8 55.5 %all-gather.15.cloned.1.call-done = bf16[4096,1024]{1,0:T(8,128)(2,1)} async-done(((bf16[1024,1024]{1,0:T(8,128)(2,1)}), bf16[4096,1024]{1,0:T(8,128)(2,1)}) %all-gather.15.cloned.1.call-update) | async-done | bytes 8388624 | tf_op jit(solution)/shard_map/all_gather | solution.py:170
  233.2 7.4 reduce_sum.219
  258.6 9.2 all-gather.11.cloned.1.call-done
  267.8 15.5 %multiply_convert_fusion = (bf16[1024,1024]{1,0:T(8,128)(2,1)}, f32[1024,1024]{1,0:T(8,128)}, f32[1024,1024]{1,0:T(8,128)}) fusion(f32[1024]{0:T(1024)S(1)} %copy-done.48, bf16[1024,1024]{1,0:T(8,128)(2,1)} %all-gather.11.cloned.1.call-done, f32[1024,1024]{1,0:T(8,128)} %add_subtract_fusion, f32[1024]{0:T(1024)S(1)} %copy-done.43, f32[1024]{0:T(1024)S(1)} %copy-done.33, ...), kind=kOutput, calls=%fused_computation.69 | convolution fusion | flops 2220883968 | bytes 16793600 | tf_op jit(solution)/shard_map/dot_general | solution.py:179
  283.3 19.0 %all-gather.13.cloned.1.call-done = bf16[1024,1024]{1,0:T(8,128)(2,1)} async-done(((bf16[512,1024]{1,0:T(8,128)(2,1)}), bf16[1024,1024]{1,0:T(8,128)(2,1)}) %all-gather.13.cloned.1.call-update) | async-done | bytes 2097168 | tf_op jit(solution)/shard_map/all_gather | solution.py:177
  302.3 5.9 convolution_convert_fusion.1
  308.9 21.3 %psum.114 = f32[]{:T(128)} all-reduce(f32[]{:T(128)} %convert_reduce_fusion.5), channel_id=1, replica_groups=mesh['shard'=2,'ctx'=4,'tensor'=4] {'shard','ctx'}, use_global_device_ids=true, to_apply=%region_13.14 | all-reduce | flops 1 | bytes 8 | tf_op jit(solution)/shard_map/psum | solution.py:189
  335.5 24.3 %all-reduce.6.cloned.1.call-done = bf16[1024,1024]{1,0:T(8,128)(2,1)} async-done(((bf16[1024,1024]{1,0:T(8,128)(2,1)}), bf16[1024,1024]{1,0:T(8,128)(2,1)}) %all-reduce.6.cloned.1.call-update) | async-done | bytes 2097168 | tf_op jit(solution)/shard_map/psum | solution.py:183
  366.0 5.8 multiply_reduce_fusion
  387.3 51.5 %all-reduce.8.cloned.1.call-done = bf16[1024,1024]{1,0:T(8,128)(2,1)} async-done(((bf16[1024,1024]{1,0:T(8,128)(2,1)}), bf16[1024,1024]{1,0:T(8,128)(2,1)}) %all-reduce.8.cloned.1.call-update) | async-done | bytes 2097168 | tf_op jit(solution)/shard_map/psum | solution.py:200
  455.9 7.8 multiply_reduce_fusion.7
  466.6 25.0 %while.29 = (s32[]{:T(128)}, f32[256,4,4,64]{0,3,2,1:T(8,128)}, bf16[2,512,4,512]{1,3,2,0:T(8,128)(2,1)}, bf16[2,512,4,4,64]{1,4,3,2,0:T(8,128)(2,1)S(1)}, bf16[...) while((s32[]{:T(128)}, f32[256,4,4,64]{0,3,2,1:T(8,128)}, ...), condition=%wide.region_21.22_spmd.clone, body=%wide.region_20.21_spmd.clone.sunk | while | flops 1364983808 | bytes 76595896 | solution.py:223
  491.6 7.3 copy.94
  505.1 70.8 %reduce-scatter.8.cloned.1.call-done = bf16[256,4,512]{2,0,1:T(8,128)(2,1)} async-done(((bf16[1024,4,512]{2,0,1:T(8,128)(2,1)}), bf16[256,4,512]{2,0,1:T(8,128)(2,1)}) %reduce-scatter.8.cloned.1.call-update) | async-done | bytes 1048592 | tf_op jit(solution)/shard_map/reduce_scatter | solution.py:225
  581.9 5.5 add_convert_fusion
  587.5 52.0 %all-reduce.10.cloned.1.call-done = bf16[1024,1024]{1,0:T(8,128)(2,1)} async-done(((bf16[1024,1024]{1,0:T(8,128)(2,1)}), bf16[1024,1024]{1,0:T(8,128)(2,1)}) %all-reduce.10.cloned.1.call-update) | async-done | bytes 2097168 | tf_op jit(solution)/shard_map/psum | solution.py:239
  663.6 7.4 fusion.63
  671.2 6.6 fusion.79
  690.6 38.8 %all-reduce = (f32[]{:T(128)}, f32[1024]{0:T(1024)}, f32[256]{0:T(256)}, f32[256]{0:T(256)}, f32[1024]{0:T(1024)}, /*index=5*/f32[1024]{0:T(1024)}, f32[1024]{0:...) all-reduce(f32[]{:T(128)} %get-tuple-element.280, ...), channel_id=1, replica_groups=mesh['shard'=2,'ctx'=4,'tensor'=4] {'shard','ctx'}, use_global_device_ids=true, to_apply=%region_11.12 | all-reduce | flops 8705 | bytes 69640 | tf_op jit(solution)/shard_map/psum | solution.py:189
  735.5 64.8 %reduce-scatter.10.cloned.1.call-done = f32[128,256]{1,0:T(8,128)} async-done(((f32[1024,256]{1,0:T(8,128)}), f32[128,256]{1,0:T(8,128)}) %reduce-scatter.10.cloned.1.call-update) | async-done | bytes 131088 | tf_op jit(solution)/shard_map/reduce_scatter | solution.py:276
  800.3 66.4 %reduce-scatter.16.cloned.1.call-done = f32[128,256]{1,0:T(8,128)} async-done(((f32[1024,256]{1,0:T(8,128)}), f32[128,256]{1,0:T(8,128)}) %reduce-scatter.16.cloned.1.call-update) | async-done | bytes 131088 | tf_op jit(solution)/shard_map/reduce_scatter | solution.py:279
  866.7 91.6 %reduce-scatter.18.cloned.1.call-done = f32[128,1024]{1,0:T(8,128)} async-done(((f32[1024,1024]{1,0:T(8,128)}), f32[128,1024]{1,0:T(8,128)}) %reduce-scatter.18.cloned.1.call-update) | async-done | bytes 524304 | tf_op jit(solution)/shard_map/reduce_scatter | solution.py:280
  958.3 91.8 %reduce-scatter.20.cloned.1.call-done = f32[128,1024]{1,0:T(8,128)} async-done(((f32[1024,1024]{1,0:T(8,128)}), f32[128,1024]{1,0:T(8,128)}) %reduce-scatter.20.cloned.1.call-update) | async-done | bytes 524304 | tf_op jit(solution)/shard_map/reduce_scatter | solution.py:281
  1050.1 67.3 %reduce-scatter.14.cloned.1.call-done = f32[128,256]{1,0:T(8,128)} async-done(((f32[1024,256]{1,0:T(8,128)}), f32[128,256]{1,0:T(8,128)}) %reduce-scatter.14.cloned.1.call-update) | async-done | bytes 131088 | tf_op jit(solution)/shard_map/reduce_scatter | solution.py:278
  1117.4 66.4 %reduce-scatter.12.cloned.1.call-done = f32[128,256]{1,0:T(8,128)} async-done(((f32[1024,256]{1,0:T(8,128)}), f32[128,256]{1,0:T(8,128)}) %reduce-scatter.12.cloned.1.call-update) | async-done | bytes 131088 | tf_op jit(solution)/shard_map/reduce_scatter | solution.py:277
  (253 shorter events, 225.3 us)
Async XLA Ops:
  7.2 73.8 %all-gather.7.cloned.1.call-start = ((), (), s32[]{:S(2)}) async-start(), calls=%async_computation.7 | async-start | bytes 2621440 | tf_op jit(solution)/shard_map/all_gather | solution.py:160
  18.7 14.5 %copy-start.30 = (bf16[512,256]{1,0:T(8,128)(2,1)S(1)}, bf16[512,256]{1,0:T(8,128)(2,1)}, u32[]{:S(2)}) copy-start(bf16[512,256]{1,0:T(8,128)(2,1)} %param.34) | copy-start | bytes 786436
  28.7 12.6 %copy-start.16 = (bf16[1024,256]{1,0:T(8,128)(2,1)}, bf16[1024,256]{1,0:T(8,128)(2,1)S(1)}, u32[]{:S(2)}) copy-start(bf16[1024,256]{1,0:T(8,128)(2,1)S(1)} %all_gather.32) | copy-start | bytes 1572868
  28.7 13.4 %copy-start.44 = (f32[256]{0:T(256)S(1)}, f32[256]{0:T(256)}, u32[]{:S(2)}) copy-start(f32[256]{0:T(256)} %param.35) | copy-start | bytes 3076
  33.1 13.4 %copy-start.31 = (bf16[512,256]{1,0:T(8,128)(2,1)S(1)}, bf16[512,256]{1,0:T(8,128)(2,1)}, u32[]{:S(2)}) copy-start(bf16[512,256]{1,0:T(8,128)(2,1)} %param.31) | copy-start | bytes 786436
  33.1 94.5 %all-gather.9.cloned.1.call-start = ((), (), s32[]{:S(2)}) async-start(), calls=%async_computation.8 | async-start | bytes 2621440 | tf_op jit(solution)/shard_map/all_gather | solution.py:161
  42.1 11.8 copy-start.45
  46.4 186.8 %all-gather.15.cloned.1.call-start = ((), (), s32[]{:S(2)}) async-start(), calls=%async_computation.22 | async-start | bytes 10485760 | tf_op jit(solution)/shard_map/all_gather | solution.py:170
  176.6 91.2 %all-gather.11.cloned.1.call-start = ((), (), s32[]{:S(2)}) async-start(), calls=%async_computation.9 | async-start | bytes 3145728 | tf_op jit(solution)/shard_map/all_gather | solution.py:176
  177.1 125.2 %all-gather.13.cloned.1.call-start = ((), (), s32[]{:S(2)}) async-start(), calls=%async_computation.10 | async-start | bytes 3145728 | tf_op jit(solution)/shard_map/all_gather | solution.py:177
  177.7 182.1 %all-reduce.6.cloned.1.call-start = ((), (), s32[]{:S(2)}) async-start(), calls=%async_computation.11 | async-start | bytes 4194304 | tf_op jit(solution)/shard_map/psum | solution.py:183
  255.9 11.9 copy-start.33
  255.9 11.9 copy-start.43
  255.9 11.9 copy-start.48
  308.2 51.6 %copy-start.41 = (f32[1024]{0:T(1024)S(1)}, f32[1024]{0:T(1024)}, u32[]{:S(2)}) copy-start(f32[1024]{0:T(1024)} %param.43) | copy-start | bytes 12292
  308.3 130.6 %all-reduce.8.cloned.1.call-start = ((), (), s32[]{:S(2)}) async-start(), calls=%async_computation.12 | async-start | bytes 4194304 | tf_op jit(solution)/shard_map/psum | solution.py:200
  387.2 188.7 %reduce-scatter.8.cloned.1.call-start = ((), (), s32[]{:S(2)}) async-start(), calls=%async_computation.13 | async-start | bytes 5242880 | tf_op jit(solution)/shard_map/reduce_scatter | solution.py:225
  438.8 6.5 copy-start.8
  438.8 7.1 copy-start.15
  498.9 140.6 %all-reduce.10.cloned.1.call-start = ((), (), s32[]{:S(2)}) async-start(), calls=%async_computation.14 | async-start | bytes 4194304 | tf_op jit(solution)/shard_map/psum | solution.py:239
  502.4 75.3 %copy-start.17 = (bf16[1024,256]{1,0:T(8,128)(2,1)S(1)}, bf16[1024,256]{1,0:T(8,128)(2,1)}, u32[]{:S(2)}) copy-start(bf16[1024,256]{1,0:T(8,128)(2,1)} %copy-done.16) | copy-start | bytes 1572868
  587.4 145.5 %all-reduce.12.cloned.1.call-start = ((), (), s32[]{:S(2)}) async-start(), calls=%async_computation.15 | async-start | bytes 2097152 | tf_op jit(solution)/shard_map/psum | solution.py:259
  654.6 145.7 %reduce-scatter.10.cloned.1.call-start = ((), (), s32[]{:S(2)}) async-start(), calls=%async_computation.16 | async-start | bytes 1179648 | tf_op jit(solution)/shard_map/reduce_scatter | solution.py:276
  660.1 206.5 %reduce-scatter.16.cloned.1.call-start = ((), (), s32[]{:S(2)}) async-start(), calls=%async_computation.19 | async-start | bytes 1179648 | tf_op jit(solution)/shard_map/reduce_scatter | solution.py:279
  663.5 294.8 %reduce-scatter.18.cloned.1.call-start = ((), (), s32[]{:S(2)}) async-start(), calls=%async_computation.20 | async-start | bytes 4718592 | tf_op jit(solution)/shard_map/reduce_scatter | solution.py:280
  671.0 379.1 %reduce-scatter.20.cloned.1.call-start = ((), (), s32[]{:S(2)}) async-start(), calls=%async_computation.21 | async-start | bytes 4718592 | tf_op jit(solution)/shard_map/reduce_scatter | solution.py:281
  677.8 439.5 %reduce-scatter.14.cloned.1.call-start = ((), (), s32[]{:S(2)}) async-start(), calls=%async_computation.18 | async-start | bytes 1179648 | tf_op jit(solution)/shard_map/reduce_scatter | solution.py:278
  683.9 6.6 copy-start.36
  684.0 6.6 copy-start.37
  684.0 6.6 copy-start.38
  684.0 499.8 %reduce-scatter.12.cloned.1.call-start = ((), (), s32[]{:S(2)}) async-start(), calls=%async_computation.17 | async-start | bytes 1179648 | tf_op jit(solution)/shard_map/reduce_scatter | solution.py:277
  684.0 499.7 %copy-start.1 = (bf16[256,1024]{1,0:T(8,128)(2,1)S(1)}, bf16[256,1024]{1,0:T(8,128)(2,1)}, u32[]{:S(2)}) copy-start(bf16[256,1024]{1,0:T(8,128)(2,1)} %param.29) | copy-start | bytes 1572868
  (39 other events, 134.2 us)
Sparse Core Ops, SparseCore 0:
  33.2 47.7 all-gather.6
  83.1 44.4 all-gather.8
  176.7 56.5 all-gather.14
  234.6 33.1 all-gather.10
  269.2 33.1 all-gather.12
  308.4 51.3 all-reduce.5
  387.3 51.4 all-reduce.7
  499.1 76.8 reduce-scatter.7
  587.6 51.8 all-reduce.9
  654.8 78.1 all-reduce.11
  737.3 62.8 reduce-scatter.9
  804.1 62.5 reduce-scatter.15
  871.3 86.9 reduce-scatter.17
  962.4 87.6 reduce-scatter.19
  1054.3 63.0 reduce-scatter.13
  1121.2 62.5 reduce-scatter.11
